TPU v7x, 256 devices: a whole 4x4x8 slice. The times are simulated.
256 devices in a mesh: row: 8 (over y, core), col: 32 (over x, z).
Axes of the slice: x: 4, y: 4, z: 8, core: 2. Of those that a mesh axis runs over, the one named last changes fastest.
Arguments:
- sources: float32 [65536, 256], P(('row', 'col')), may hold values from -6 to 6
- targets: float32 [65536, 256], P(('col', 'row')), may hold values from -6 to 6
- g_pot: float32 [65536], P(('col', 'row')), may hold values from -1 to 12
- log_a: float32 [65536], P(('row', 'col')), may hold values from -14 to -8
- log_b: float32 [65536], P(('col', 'row')), may hold values from -14 to -8
- src_block: int32 [16384], P(('row', 'col')), may hold values from 0 to 31, as said below
- tgt_block: int32 [16384], P(('row', 'col')), may hold values from 0 to 7, as said below
- pair_count: int32 [256], P(('row', 'col')), may hold values from 16 to 64, as said below
Outputs:
- f_new: float32 [65536], P(('row', 'col'))
- g_new: float32 [65536], P(('col', 'row'))
Inputs may be any that keep to these rules, and one draw needn't show every extreme that they name: `src_block`: within each row index, slot 0 of the 32 devices names together every source block of that row index once; slot k and slot k + 32 of a device name the same source block. `tgt_block`: within each col index, slot 0 of the 8 devices names together every target block of that col index once. `pair_count`: some device has all 64 slots live.
All inputs are finite; a program needn't handle non-finite values.
Results may differ from a plain program's by a relative error of at most 0.0003.
Values sent between devices are 32-bit elements; how exact they have to be, the bound alone decides.
A program may use at most 128 MiB of HBM per device.

v0:
```python
import jax
import jax.numpy as jnp
from jax import lax
from jax.sharding import PartitionSpec as P

BLK = 256
entropy = 0.05
lowest = -1e30


def squares_of(rows):
    return jnp.sum(rows * rows, axis=-1)


def cost_blocks(src_rows, tgt_rows, src_sq, tgt_sq):
    inner = jnp.einsum("kid,kjd->kij", src_rows, tgt_rows, precision=lax.Precision.HIGHEST)
    return (src_sq[:, :, None] + tgt_sq[:, None, :] - 2.0 * inner) / src_rows.shape[2]


def fold_blocks(slot_top, slot_total, slot_ids, alive, count):
    onehot = (slot_ids[:, None] == jnp.arange(count, dtype=jnp.int32)[None, :]) & alive[:, None]
    masked = jnp.where(onehot.T[:, :, None], slot_top[None, :, :], lowest)
    top = jnp.max(masked, axis=1)
    back = jnp.take(top, slot_ids, axis=0)
    weighted = jnp.where(alive[:, None], slot_total * jnp.exp(slot_top - back), 0.0)
    total = jnp.dot(onehot.T.astype(jnp.float32), weighted, precision=lax.Precision.HIGHEST)
    return (top.reshape(-1), total.reshape(-1))


def local(sources, targets, g_pot, log_a, log_b, src_block, tgt_block, pair_count):
    used_pairs = pair_count[0]
    slots = src_block.shape[0]
    alive = jnp.arange(slots, dtype=jnp.int32) < used_pairs
    tgt_all, pot_all = (
        lax.all_gather(targets, "row", axis=0, tiled=True),
        lax.all_gather(g_pot, "row", axis=0, tiled=True),
    )
    src_all, weight_all = (
        lax.all_gather(sources, "col", axis=0, tiled=True),
        lax.all_gather(log_a, "col", axis=0, tiled=True),
    )
    width = sources.shape[1]
    src_count = src_all.shape[0] // BLK
    tgt_count = tgt_all.shape[0] // BLK
    src_blocks = src_all.reshape(src_count, BLK, width)
    tgt_blocks = tgt_all.reshape(tgt_count, BLK, width)
    src_sq_all = squares_of(src_blocks)
    tgt_sq_all = squares_of(tgt_blocks)
    src_rows = jnp.take(src_blocks, src_block, axis=0)
    tgt_rows = jnp.take(tgt_blocks, tgt_block, axis=0)
    src_sq = jnp.take(src_sq_all, src_block, axis=0)
    tgt_sq = jnp.take(tgt_sq_all, tgt_block, axis=0)
    pot_rows = jnp.take(pot_all.reshape(tgt_count, BLK), tgt_block, axis=0)
    costs = cost_blocks(src_rows, tgt_rows, src_sq, tgt_sq)
    scores = (pot_rows[:, None, :] - costs) / entropy
    slot_top = jnp.max(scores, axis=2)
    slot_total = jnp.sum(jnp.exp(scores - slot_top[:, :, None]), axis=2)
    src_top, src_total = fold_blocks(slot_top, slot_total, src_block, alive, src_count)
    whole_top = lax.pmax(src_top, "col")
    src_total = lax.psum(src_total * jnp.exp(src_top - whole_top), "col")
    src_top = whole_top
    f_all = entropy * weight_all - entropy * (src_top + jnp.log(src_total))
    second_costs = cost_blocks(src_rows, tgt_rows, src_sq, tgt_sq)
    f_rows = jnp.take(f_all.reshape(src_count, BLK), src_block, axis=0)
    back_scores = (f_rows[:, :, None] - second_costs) / entropy
    col_top = jnp.max(back_scores, axis=1)
    col_total = jnp.sum(jnp.exp(back_scores - col_top[:, None, :]), axis=1)
    tgt_top, tgt_total = fold_blocks(col_top, col_total, tgt_block, alive, tgt_count)
    whole_tgt = lax.pmax(tgt_top, "row")
    tgt_total = lax.psum(tgt_total * jnp.exp(tgt_top - whole_tgt), "row")
    tgt_top = whole_tgt
    own_src = sources.shape[0]
    own_tgt = targets.shape[0]
    f_own = lax.dynamic_slice_in_dim(f_all, lax.axis_index("col") * own_src, own_src, 0)
    tgt_offset = lax.axis_index("row") * own_tgt
    top_own = lax.dynamic_slice_in_dim(tgt_top, tgt_offset, own_tgt, 0)
    total_own = lax.dynamic_slice_in_dim(tgt_total, tgt_offset, own_tgt, 0)
    g_own = entropy * log_b - entropy * (top_own + jnp.log(total_own))
    return (f_own, g_own)


def solution(mesh):
    placed = (
        P(("row", "col"), None),
        P(("col", "row"), None),
        P(("col", "row")),
        P(("row", "col")),
        P(("col", "row")),
        P(("row", "col")),
        P(("row", "col")),
        P(("row", "col")),
    )
    return jax.shard_map(
        local,
        mesh=mesh,
        in_specs=placed,
        out_specs=(P(("row", "col")), P(("col", "row"))),
        check_vma=False,
    )
```

profile of v0, /device:TPU:1, one launch (start us, length us, event | category | flops | bytes accessed | tf_op | source)
XLA Modules:
  0.0 527.1 jit_solution(1191801241612126786)
XLA Ops:
  7.2 0.0 all-gather.7.cloned.1.call-start
  7.2 0.7 all-gather.7.cloned.1.call-update
  7.9 0.0 all-gather.5.cloned.1.call-start
  7.9 0.7 all-gather.5.cloned.1.call-update
  8.7 12.4 %all-gather.1 = f32[8,1,256]{2,1,0:T(1,128)S(1)} all-gather(f32[1,1,256]{2,1,0:T(1,128)} %bitcast.32), channel_id=1, replica_groups=mesh['row'=8,'col'=32] {'row'}, dimensions={0}, use_global_device_ids=true | all-gather | bytes 9216 | tf_op jit(solution)/shard_map/all_gather | solution.py:36
  21.7 0.7 compare_select_fusion.1
  22.4 0.7 gather_fusion.2
  23.0 37.7 %all-gather = f32[32,1,256]{2,1,0:T(1,128)S(1)} all-gather(f32[1,1,256]{2,1,0:T(1,128)} %bitcast.33), channel_id=1, replica_groups=mesh['row'=8,'col'=32] {'col'}, dimensions={0}, use_global_device_ids=true | all-gather | bytes 33792 | tf_op jit(solution)/shard_map/all_gather | solution.py:40
  60.8 0.7 compare_select_fusion
  61.4 0.7 compare_and_fusion.1
  62.1 0.7 compare_and_fusion
  62.8 0.7 fusion.37
  63.4 0.7 fusion.36
  64.1 0.0 all-gather.7.cloned.1.call-done
  64.2 1.9 multiply_reduce_fusion.1
  66.1 0.7 gather_fusion.4
  66.8 10.5 %gather_fusion.1 = f32[64,256,256]{2,1,0:T(8,128)} fusion(f32[8,256,256]{2,1,0:T(8,128)} %bitcast.20, s32[1024]{0:T(1024)S(1)} %pad_clamp_fusion.1), kind=kCustom, calls=%fused_computation.7 | custom fusion | bytes 33554688 | tf_op jit(solution)/shard_map/jit(_take)/gather | solution.py:50
  77.3 0.1 broadcast_select_fusion.3
  77.3 64.3 %all-gather.5.cloned.1.call-done = f32[8192,256]{1,0:T(8,128)} async-done(((f32[256,256]{1,0:T(8,128)}), f32[8192,256]{1,0:T(8,128)}) %all-gather.5.cloned.1.call-update) | async-done | bytes 8388624 | tf_op jit(solution)/shard_map/all_gather | solution.py:39
  141.6 4.5 multiply_reduce_fusion
  146.2 0.7 gather_fusion.3
  146.8 11.6 %gather_fusion = f32[64,256,256]{2,1,0:T(8,128)} fusion(f32[32,256,256]{2,1,0:T(8,128)} %bitcast.21, s32[1024]{0:T(1024)S(1)} %pad_clamp_fusion), kind=kCustom, calls=%fused_computation.6 | custom fusion | bytes 33554688 | tf_op jit(solution)/shard_map/jit(_take)/gather | solution.py:49
  158.5 0.1 broadcast_select_fusion.2
  158.5 29.9 %fusion.3 = (f32[64,256]{1,0:T(8,128)S(1)}, f32[64,256,256]{2,1,0:T(8,128)}) fusion(f32[64,256]{1,0:T(8,128)S(1)} %get-tuple-element.4, f32[64,256,256]{2,1,0:T(8,128)} %gather_fusion.1, pred[64]{0:T(512)(128)(4,1)S(1)} %compare_and_fusion.1, f32[64,256,256]{2,1,0:T(8,128)} %gather_fusion, pred[64]{0:T(512)(128)(4,1)S(1)} %compare_and_fusion, ...), kind=kOutput, calls=%fused_computation.16 | convolution fusion | flops 12922634240 | bytes 50593920 | tf_op jit(solution)/shard_map/kid,kjd->kij/dot_general | solution.py:16
  188.4 0.0 copy-start.1
  188.4 8.5 %exponential_reduce_fusion.1 = f32[64,256]{1,0:T(8,128)S(1)} fusion(f32[64,256,256]{2,1,0:T(8,128)} %get-tuple-element.7, f32[64,256]{1,0:T(8,128)S(1)} %get-tuple-element.6, f32[64,256]{1,0:T(8,128)S(1)} %get-tuple-element.4), kind=kLoop, calls=%fused_computation.10 | loop fusion | flops 16760832 | bytes 16973824 | tf_op jit(solution)/shard_map/reduce_sum | solution.py:57
  197.0 0.5 select_reduce_fusion
  197.5 0.7 gather_fusion.5
  198.2 0.0 copy-done.1
  198.2 0.3 convolution_bitcast_fusion
  198.5 111.5 %pmax.14 = f32[8192]{0:T(1024)S(1)} all-reduce(f32[8192]{0:T(1024)S(1)} %bitcast.25), channel_id=1, replica_groups=mesh['row'=8,'col'=32] {'col'}, use_global_device_ids=true, to_apply=%region_4.7 | all-reduce | flops 8192 | bytes 65536 | tf_op jit(solution)/shard_map/pmax | solution.py:59
  310.0 110.7 %psum.14 = f32[8192]{0:T(1024)S(1)} all-reduce(f32[8192]{0:T(1024)S(1)} %exponential_multiply_fusion), channel_id=1, replica_groups=mesh['row'=8,'col'=32] {'col'}, use_global_device_ids=true, to_apply=%region_6.9 | all-reduce | flops 8192 | bytes 65536 | tf_op jit(solution)/shard_map/psum | solution.py:60
  420.8 0.7 gather_fusion.6
  421.4 0.1 broadcast_select_fusion
  421.5 0.0 copy-start.2
  421.5 0.0 copy-start
  421.5 7.2 %fusion.4 = f32[64,256]{1,0:T(8,128)S(1)} fusion(f32[64,256,256]{2,1,0:T(8,128)} %get-tuple-element.7, f32[64,256]{1,0:T(8,128)S(1)} %broadcast_select_fusion), kind=kLoop, calls=%fused_computation.17 | loop fusion | flops 12566528 | bytes 16908288 | tf_op jit(solution)/shard_map/reduce_max | solution.py:66
  428.8 8.0 %exponential_reduce_fusion = f32[64,256]{1,0:T(8,128)S(1)} fusion(f32[64,256,256]{2,1,0:T(8,128)} %get-tuple-element.7, f32[64,256]{1,0:T(8,128)S(1)} %fusion.4, f32[64,256]{1,0:T(8,128)S(1)} %broadcast_select_fusion), kind=kLoop, calls=%fused_computation.8 | loop fusion | flops 16760832 | bytes 16973824 | tf_op jit(solution)/shard_map/reduce_sum | solution.py:67
  436.8 0.1 select_reduce_fusion.1
  437.0 0.7 gather_fusion.7
  437.6 0.0 copy-done.2
  437.6 0.3 convolution_bitcast_fusion.1
  437.9 68.4 %pmax.15 = f32[2048]{0:T(1024)S(1)} all-reduce(f32[2048]{0:T(1024)S(1)} %bitcast.29), channel_id=1, replica_groups=mesh['row'=8,'col'=32] {'row'}, use_global_device_ids=true, to_apply=%region_9.12 | all-reduce | flops 2048 | bytes 16384 | tf_op jit(solution)/shard_map/pmax | solution.py:69
  506.3 12.7 %psum.15 = f32[2048]{0:T(1024)S(1)} all-reduce(f32[2048]{0:T(1024)S(1)} %exponential_multiply_fusion.1), channel_id=1, replica_groups=mesh['row'=8,'col'=32] {'row'}, use_global_device_ids=true, to_apply=%region_11.14 | all-reduce | flops 2048 | bytes 16384 | tf_op jit(solution)/shard_map/psum | solution.py:70
  519.0 0.6 dynamic_slice.9
  519.7 0.0 copy-done
  519.7 0.6 multiply_subtract_fusion.1
  (15 shorter events, 0.2 us)
Async XLA Ops:
  7.2 57.0 %all-gather.7.cloned.1.call-start = ((), (), s32[]{:S(2)}) async-start(), calls=%async_computation.1 | async-start | bytes 2359296 | tf_op jit(solution)/shard_map/all_gather | solution.py:35
  7.9 133.7 %all-gather.5.cloned.1.call-start = ((), (), s32[]{:S(2)}) async-start(), calls=%async_computation | async-start | bytes 8650752 | tf_op jit(solution)/shard_map/all_gather | solution.py:39
  188.4 9.7 %copy-start.1 = (s32[64]{0:T(128)S(1)}, s32[64]{0:T(128)}, u32[]{:S(2)}) copy-start(s32[64]{0:T(128)} %param.17) | copy-start | bytes 772
  421.5 16.1 %copy-start.2 = (s32[64]{0:T(128)S(1)}, s32[64]{0:T(128)}, u32[]{:S(2)}) copy-start(s32[64]{0:T(128)} %param.18) | copy-start | bytes 772
  421.5 98.1 %copy-start = (f32[256]{0:T(256)S(1)}, f32[256]{0:T(256)}, u32[]{:S(2)}) copy-start(f32[256]{0:T(256)} %param.16) | copy-start | bytes 3076
Sparse Core Ops, SparseCore 0:
  9.8 32.0 all-gather.6
  44.5 97.0 all-gather.4
where the time goes:
time: 528 us; the launch traced here: 527 us
  blocking collectives  353 us (67%)
  waiting for transfers between devices  65.7 us (12%)
  other arithmetic  35.9 us (7%)
  matrix products  30.4 us (6%)
  local copies, waits for them, and re-layouts  26.8 us (5%)
  between operations  14.9 us (3%)
    pmax x1, blocking collectives, local(): whole_top = lax.pmax(src_top, 'col')  112 us
    psum x1, blocking collectives, local(): src_total = lax.psum(src_total * jnp.exp(src_top - whole_top), 'col')  111 us
    pmax x1, blocking collectives, local(): whole_tgt = lax.pmax(tgt_top, 'row')  68.4 us
    all_gather x1, waiting for transfers between devices, local(): lax.all_gather(sources, 'col', axis=0, tiled=True)  64.3 us
    all_gather x1, blocking collectives, local(): lax.all_gather(log_a, 'col', axis=0, tiled=True)  37.7 us
    dot_general x1, matrix products, cost_blocks(): jnp.einsum('kid,kjd->kij', src_rows, tgt_rows, precision=lax.Precision.HI...  29.9 us
    psum x1, blocking collectives, local(): tgt_total = lax.psum(tgt_total * jnp.exp(tgt_top - whole_tgt), 'row')  12.7 us
    all_gather x1, blocking collectives, local(): lax.all_gather(g_pot, 'row', axis=0, tiled=True)  12.4 us
  transfers between devices with their start and end apart: 2, of which 1 were waited for; matrix products, arithmetic and copies ran while one was open for 3% of the time, Pallas kernels for 0%

commit v1 on v0

--- a/solution.py
+++ b/solution.py
@@ -36,7 +36,10 @@
         lax.all_gather(g_pot, "row", axis=0, tiled=True),
     )
     src_all, weight_all = (
-        lax.all_gather(sources, "col", axis=0, tiled=True),
+        jnp.concatenate(
+            lax.all_to_all(jnp.stack([sources for _ in range(lax.psum(1, "col"))]), "col", 0, 0),
+            axis=0,
+        ),
         lax.all_gather(log_a, "col", axis=0, tiled=True),
     )
     width = sources.shape[1]

time: 528 us -> 647 us (1.23)
  blocking collectives: 353 us -> 525 us
  waiting for transfers between devices: 65.7 us -> 0.7 us
  starting transfers between devices: 0.08 us -> 12 us
    all_gather x1, blocking collectives: 37.7 us -> 201 us  [local(): lax.all_gather(log_a, 'col', axis=0, tiled=True)]
    all_gather x1 -> x0, waiting for transfers between devices: 64.3 us -> none  [local(): lax.all_gather(sources, 'col', axis=0, tiled=True)]
    all_to_all x0 -> x1, starting transfers between devices: none -> 12 us  [local(): lax.all_to_all(jnp.stack([sources for _ in range(lax.psum(1, 'col'))]), '...]
    pmax x1, blocking collectives: 68.4 us -> 76.2 us  [local(): whole_tgt = lax.pmax(tgt_top, 'row')]
  transfers between devices with their start and end apart: 2 -> 2, of which waited for: 1 -> 0; matrix products, arithmetic and copies ran while one was open for 3% -> 2% of each run, Pallas kernels for 0% -> 0%
where the time goes in v1:
time: 647 us
  blocking collectives  525 us (81%)
  other arithmetic  31.9 us (5%)
  local copies, waits for them, and re-layouts  31.8 us (5%)
  matrix products  30.4 us (5%)
  between operations  15 us (2%)
  starting transfers between devices  12 us (2%)
    all_gather x1, blocking collectives, local(): lax.all_gather(log_a, 'col', axis=0, tiled=True)  201 us
    pmax x1, blocking collectives, local(): whole_top = lax.pmax(src_top, 'col')  113 us
    psum x1, blocking collectives, local(): src_total = lax.psum(src_total * jnp.exp(src_top - whole_top), 'col')  111 us
    pmax x1, blocking collectives, local(): whole_tgt = lax.pmax(tgt_top, 'row')  76.2 us
    dot_general x1, matrix products, cost_blocks(): jnp.einsum('kid,kjd->kij', src_rows, tgt_rows, precision=lax.Precision.HI...  29.9 us
  transfers between devices with their start and end apart: 2, of which 0 were waited for; matrix products, arithmetic and copies ran while one was open for 2% of the time, Pallas kernels for 0%

profile of v1, /device:TPU:1, one launch (start us, length us, event | category | flops | bytes accessed | tf_op | source)
XLA Modules:
  0.0 646.6 jit_solution(660882143342436884)
XLA Ops:
  7.2 0.0 copy-start
  7.2 0.0 copy-start.4
  7.2 0.0 copy-start.1
  7.2 0.0 copy-start.3
  7.2 5.1 stack.2
  12.3 12.0 %all-to-all-start = ((f32[32,256,256]{2,1,0:T(8,128)}), f32[32,256,256]{2,1,0:T(8,128)}, u32[]{:S(2)}, u32[]{:S(2)}) async-start(f32[32,256,256]{2,1,0:T(8,128)} %stack.2), calls=%async_computation | async-start | bytes 16777216 | tf_op jit(solution)/shard_map/all_to_all | solution.py:40
  24.3 0.0 all-gather.4.cloned.1.call-start
  24.4 0.7 all-gather.4.cloned.1.call-update
  25.1 0.0 copy-done
  25.1 11.6 %all-gather.1 = f32[8,1,256]{2,1,0:T(1,128)S(1)} all-gather(f32[1,1,256]{2,1,0:T(1,128)S(1)} %bitcast.30), channel_id=1, replica_groups=mesh['row'=8,'col'=32] {'row'}, dimensions={0}, use_global_device_ids=true | all-gather | bytes 9216 | tf_op jit(solution)/shard_map/all_gather | solution.py:36
  37.4 0.0 copy-done.4
  37.4 0.7 gather_fusion.2
  38.0 0.0 copy-done.1
  38.1 200.9 %all-gather = f32[32,1,256]{2,1,0:T(1,128)S(1)} all-gather(f32[1,1,256]{2,1,0:T(1,128)S(1)} %bitcast.31), channel_id=1, replica_groups=mesh['row'=8,'col'=32] {'col'}, dimensions={0}, use_global_device_ids=true | all-gather | bytes 33792 | tf_op jit(solution)/shard_map/all_gather | solution.py:43
  239.0 0.0 copy-done.3
  239.1 0.0 all-gather.4.cloned.1.call-done
  239.2 1.9 multiply_reduce_fusion.1
  241.1 0.7 gather_fusion.4
  241.8 10.4 %gather_fusion.1 = f32[64,256,256]{2,1,0:T(8,128)} fusion(f32[8,256,256]{2,1,0:T(8,128)} %bitcast.19, s32[1024]{0:T(1024)S(1)} %pad_clamp_fusion.1), kind=kCustom, calls=%fused_computation.7 | custom fusion | bytes 33554688 | tf_op jit(solution)/shard_map/jit(_take)/gather | solution.py:53
  252.2 0.1 broadcast_select_fusion.3
  252.3 0.0 all-to-all-done
  252.3 4.5 multiply_reduce_fusion
  256.8 0.7 gather_fusion.3
  257.5 0.1 broadcast_select_fusion.2
  257.5 11.6 %gather_fusion = f32[64,256,256]{2,1,0:T(8,128)} fusion(f32[32,256,256]{2,1,0:T(8,128)} %all-to-all-done, s32[1024]{0:T(1024)S(1)} %pad_clamp_fusion), kind=kCustom, calls=%fused_computation.6 | custom fusion | bytes 33554688 | tf_op jit(solution)/shard_map/jit(_take)/gather | solution.py:52
  269.2 29.9 %fusion.3 = (f32[64,256]{1,0:T(8,128)S(1)}, f32[64,256,256]{2,1,0:T(8,128)}) fusion(f32[64,256]{1,0:T(8,128)S(1)} %get-tuple-element.4, f32[64,256,256]{2,1,0:T(8,128)} %gather_fusion.1, pred[64]{0:T(512)(128)(4,1)S(1)} %compare_and_fusion.1, f32[64,256,256]{2,1,0:T(8,128)} %gather_fusion, pred[64]{0:T(512)(128)(4,1)S(1)} %compare_and_fusion, ...), kind=kOutput, calls=%fused_computation.16 | convolution fusion | flops 12922634240 | bytes 50593920 | tf_op jit(solution)/shard_map/kid,kjd->kij/dot_general | solution.py:16
  299.1 8.5 %exponential_reduce_fusion.1 = f32[64,256]{1,0:T(8,128)S(1)} fusion(f32[64,256,256]{2,1,0:T(8,128)} %get-tuple-element.7, f32[64,256]{1,0:T(8,128)S(1)} %get-tuple-element.6, f32[64,256]{1,0:T(8,128)S(1)} %get-tuple-element.4), kind=kLoop, calls=%fused_computation.10 | loop fusion | flops 16760832 | bytes 16973824 | tf_op jit(solution)/shard_map/reduce_sum | solution.py:60
  307.6 0.5 select_reduce_fusion
  308.1 0.7 gather_fusion.5
  308.8 0.3 convolution_bitcast_fusion
  309.1 112.5 %pmax.14 = f32[8192]{0:T(1024)S(1)} all-reduce(f32[8192]{0:T(1024)S(1)} %bitcast.23), channel_id=1, replica_groups=mesh['row'=8,'col'=32] {'col'}, use_global_device_ids=true, to_apply=%region_4.7 | all-reduce | flops 8192 | bytes 65536 | tf_op jit(solution)/shard_map/pmax | solution.py:62
  421.6 110.7 %psum.14 = f32[8192]{0:T(1024)S(1)} all-reduce(f32[8192]{0:T(1024)S(1)} %exponential_multiply_fusion), channel_id=1, replica_groups=mesh['row'=8,'col'=32] {'col'}, use_global_device_ids=true, to_apply=%region_6.9 | all-reduce | flops 8192 | bytes 65536 | tf_op jit(solution)/shard_map/psum | solution.py:63
  532.4 0.7 gather_fusion.6
  533.1 0.1 broadcast_select_fusion
  533.1 0.0 copy-start.2
  533.2 7.2 %fusion.4 = f32[64,256]{1,0:T(8,128)S(1)} fusion(f32[64,256,256]{2,1,0:T(8,128)} %get-tuple-element.7, f32[64,256]{1,0:T(8,128)S(1)} %broadcast_select_fusion), kind=kLoop, calls=%fused_computation.17 | loop fusion | flops 12566528 | bytes 16908288 | tf_op jit(solution)/shard_map/reduce_max | solution.py:69
  540.4 8.0 %exponential_reduce_fusion = f32[64,256]{1,0:T(8,128)S(1)} fusion(f32[64,256,256]{2,1,0:T(8,128)} %get-tuple-element.7, f32[64,256]{1,0:T(8,128)S(1)} %fusion.4, f32[64,256]{1,0:T(8,128)S(1)} %broadcast_select_fusion), kind=kLoop, calls=%fused_computation.8 | loop fusion | flops 16760832 | bytes 16973824 | tf_op jit(solution)/shard_map/reduce_sum | solution.py:70
  548.4 0.1 select_reduce_fusion.1
  548.6 0.7 gather_fusion.7
  549.3 0.3 convolution_bitcast_fusion.1
  549.5 76.2 %pmax.15 = f32[2048]{0:T(1024)S(1)} all-reduce(f32[2048]{0:T(1024)S(1)} %bitcast.27), channel_id=1, replica_groups=mesh['row'=8,'col'=32] {'row'}, use_global_device_ids=true, to_apply=%region_9.12 | all-reduce | flops 2048 | bytes 16384 | tf_op jit(solution)/shard_map/pmax | solution.py:72
  625.8 12.7 %psum.15 = f32[2048]{0:T(1024)S(1)} all-reduce(f32[2048]{0:T(1024)S(1)} %exponential_multiply_fusion.1), channel_id=1, replica_groups=mesh['row'=8,'col'=32] {'row'}, use_global_device_ids=true, to_apply=%region_11.14 | all-reduce | flops 2048 | bytes 16384 | tf_op jit(solution)/shard_map/psum | solution.py:73
  638.4 0.6 dynamic_slice.9
  639.1 0.0 copy-done.2
  639.1 0.6 multiply_subtract_fusion.1
  (20 shorter events, 0.2 us)
Async XLA Ops:
  7.2 17.9 %copy-start = (f32[256]{0:T(256)S(1)}, f32[256]{0:T(256)}, u32[]{:S(2)}) copy-start(f32[256]{0:T(256)} %param.14) | copy-start | bytes 3076
  7.2 30.2 %copy-start.4 = (s32[64]{0:T(128)S(1)}, s32[64]{0:T(128)}, u32[]{:S(2)}) copy-start(s32[64]{0:T(128)} %param.18) | copy-start | bytes 772
  7.2 30.9 %copy-start.1 = (f32[256]{0:T(256)S(1)}, f32[256]{0:T(256)}, u32[]{:S(2)}) copy-start(f32[256]{0:T(256)} %param.15) | copy-start | bytes 3076
  7.2 231.8 %copy-start.3 = (s32[64]{0:T(128)S(1)}, s32[64]{0:T(128)}, u32[]{:S(2)}) copy-start(s32[64]{0:T(128)} %param.17) | copy-start | bytes 772
  12.3 239.9 %all-to-all-start = ((f32[32,256,256]{2,1,0:T(8,128)}), f32[32,256,256]{2,1,0:T(8,128)}, u32[]{:S(2)}, u32[]{:S(2)}) async-start(f32[32,256,256]{2,1,0:T(8,128)} %stack.2), calls=%async_computation | async-start | bytes 16777216 | tf_op jit(solution)/shard_map/all_to_all | solution.py:40
  24.3 214.8 %all-gather.4.cloned.1.call-start = ((), (), s32[]{:S(2)}) async-start(), calls=%async_computation.1 | async-start | bytes 2359296 | tf_op jit(solution)/shard_map/all_gather | solution.py:35
  533.1 105.9 %copy-start.2 = (f32[256]{0:T(256)S(1)}, f32[256]{0:T(256)}, u32[]{:S(2)}) copy-start(f32[256]{0:T(256)} %param.16) | copy-start | bytes 3076
Sparse Core Ops, SparseCore 0:
  27.0 29.9 all-gather.3
